TPU v7x, 128 devices: a whole 4x4x4 slice. The times are simulated.
128 devices in a mesh: grp: 4 (over z_hi, core), blk: 32 (over y, x, z_lo).
Axes of the slice: x: 4, y: 4, z: 4 (z_hi: 2, z_lo: 2; z = z_hi * 2 + z_lo), core: 2. Of those that a mesh axis runs over, the one named last changes fastest.
Arguments:
- targets: float32 [64, 262144], P('blk', 'grp'), may hold values from -6 to 6
- sources: float32 [128, 262144], P(('grp', 'blk')), may hold values from -6 to 6
- occupation: int32 [128], P(('grp', 'blk')), may hold values from 1 to 2
- offsets: int32 [4], replicated, may hold values from 0 to 31, as said below
Outputs:
- exchange: float32 [64, 262144], P('blk', 'grp')
Inputs may be any that keep to these rules, and one draw needn't show every extreme that they name: The groups' offsets are distinct and the largest is 31.
All inputs are finite; a program needn't handle non-finite values.
Results may differ from a plain program's by a relative error of at most 0.0003.
Values sent between devices are 32-bit elements; how exact they have to be, the bound alone decides.
No kernel may reach another device: no remote copies, remote signals or barrier semaphores. Data moves between devices by JAX's collectives and lax.ppermute only.
A program may use at most 128 MiB of HBM per device.

v0:
```python
import math

import jax
import jax.numpy as jnp
from jax import lax
from jax.sharding import PartitionSpec as P

NG = 64
STOPS = 4


box_length = 16.0
screen_square = 0.25


def shifted(block, axis, distance):
    devices = range(lax.axis_size(axis))
    route = [((i - distance) % len(devices), i) for i in devices]
    return lax.ppermute(block, axis, route)


def screened_kernel(grid_size):
    counter = jnp.arange(grid_size, dtype=jnp.int32)
    signed_freq = jnp.where(counter < grid_size // 2, counter, counter - grid_size).astype(
        jnp.float32
    )
    wave_number = 2.0 * math.pi * signed_freq / box_length
    wave_square = wave_number * wave_number
    summed = wave_square[:, None, None] + wave_square[None, :, None] + wave_square[None, None, :]
    return 4.0 * math.pi / (summed + screen_square)


def dft_table(grid_size, sign_value, factor):
    counter = jnp.arange(grid_size, dtype=jnp.int32)
    product = counter[:, None] * counter[None, :] % grid_size
    phase_angle = 2.0 * math.pi * product.astype(jnp.float32) / grid_size
    cosine = jnp.cos(phase_angle) * factor
    sine_part = jnp.sin(phase_angle) * factor
    upper_rows = jnp.stack([cosine, -sign_value * sine_part], axis=1)
    lower_rows = jnp.stack([sign_value * sine_part, cosine], axis=1)
    return jnp.stack([upper_rows, lower_rows], axis=0)


def transform(grid_field, dft_matrix):
    for repeat_index in range(3):
        grid_field = jnp.einsum(
            "qmpa,zpabc->zqbcm", dft_matrix, grid_field, precision=lax.Precision.HIGHEST
        )
    return grid_field


def exchange_terms(target_rows, source_rows, kernel_grid, forward_table, inverse_table):
    target_count, cell_count = target_rows.shape
    source_count = source_rows.shape[0]
    density = (target_rows[:, None, :] * source_rows[None, :, :]).reshape(
        target_count * source_count, NG, NG, NG
    )
    half_count = density.shape[0] // 2
    packed = jnp.stack([density[:half_count], density[half_count:]], axis=1)
    both_parts = transform(transform(packed, forward_table) * kernel_grid, inverse_table)
    potential = jnp.concatenate([both_parts[:, 0], both_parts[:, 1]], axis=0)
    potential = potential.reshape(target_count, source_count, cell_count)
    return jnp.sum(potential * source_rows[None, :, :], axis=1)


def local(targets, sources, occupation, offsets):
    whole_targets = lax.all_gather(targets, "grp", axis=1, tiled=True)
    scaled = sources * jnp.sqrt(occupation.astype(jnp.float32) * 0.5)[:, None]
    group_offset = lax.dynamic_index_in_dim(offsets, lax.axis_index("grp"), 0, keepdims=False)
    carried = scaled
    for bit_number in range(lax.axis_size("blk").bit_length() - 1):
        moved_rows = shifted(carried, "blk", 1 << bit_number)
        carried = jnp.where(group_offset // (1 << bit_number) % 2 == 1, moved_rows, carried)
    kernel_grid = screened_kernel(NG)
    forward_table = dft_table(NG, -1.0, 1.0)
    inverse_table = dft_table(NG, 1.0, 1.0 / NG)
    accumulated = jnp.zeros(whole_targets.shape, jnp.float32)
    visiting = carried
    for stop_index in range(STOPS):
        if stop_index > 0:
            visiting = shifted(visiting, "blk", 1)
        accumulated = accumulated + exchange_terms(
            whole_targets, visiting, kernel_grid, forward_table, inverse_table
        )
    summed = lax.psum_scatter(accumulated, "grp", scatter_dimension=1, tiled=True)
    return -summed


def solution(mesh):
    in_specs = (P("blk", "grp"), P(("grp", "blk"), None), P(("grp", "blk")), P())
    out_specs = P("blk", "grp")
    return jax.shard_map(local, mesh=mesh, in_specs=in_specs, out_specs=out_specs, check_vma=False)
```

profile of v0, /device:TPU:1, one launch (start us, length us, event | category | flops | bytes accessed | tf_op | source)
XLA Modules:
  0.0 639.9 jit_solution(16692638249242075791)
XLA Ops:
  9.0 2.5 collective-permute-start
  14.5 24.6 %collective-permute-done = f32[1,262144]{1,0:T(1,128)S(1)} collective-permute-done((f32[1,262144]{1,0:T(1,128)S(1)}, f32[1,262144]{1,0:T(1,128)S(1)}, u32[]{:S(2)}, u32[]{:S(2)}) %collective-permute-start) | collective-permute-done | bytes 1048608 | tf_op jit(solution)/shard_map/ppermute | solution.py:19
  41.9 26.1 %collective-permute-done.1 = f32[1,262144]{1,0:T(1,128)S(1)} collective-permute-done((f32[1,262144]{1,0:T(1,128)S(1)}, f32[1,262144]{1,0:T(1,128)S(1)}, u32[]{:S(2)}, u32[]{:S(2)}) %collective-permute-start.1) | collective-permute-done | bytes 1048608 | tf_op jit(solution)/shard_map/ppermute | solution.py:19
  69.3 26.1 %collective-permute-done.2 = f32[1,262144]{1,0:T(1,128)S(1)} collective-permute-done((f32[1,262144]{1,0:T(1,128)S(1)}, f32[1,262144]{1,0:T(1,128)S(1)}, u32[]{:S(2)}, u32[]{:S(2)}) %collective-permute-start.2) | collective-permute-done | bytes 1048608 | tf_op jit(solution)/shard_map/ppermute | solution.py:19
  96.6 22.7 %collective-permute-done.3 = f32[1,262144]{1,0:T(1,128)S(1)} collective-permute-done((f32[1,262144]{1,0:T(1,128)S(1)}, f32[1,262144]{1,0:T(1,128)S(1)}, u32[]{:S(2)}, u32[]{:S(2)}) %collective-permute-start.3) | collective-permute-done | bytes 1048608 | tf_op jit(solution)/shard_map/ppermute | solution.py:19
  120.6 22.1 %collective-permute-done.4 = f32[1,262144]{1,0:T(1,128)S(1)} collective-permute-done((f32[1,262144]{1,0:T(1,128)S(1)}, f32[1,262144]{1,0:T(1,128)S(1)}, u32[]{:S(2)}, u32[]{:S(2)}) %collective-permute-start.4) | collective-permute-done | bytes 1048608 | tf_op jit(solution)/shard_map/ppermute | solution.py:19
  144.0 23.9 %collective-permute-done.5 = f32[1,262144]{1,0:T(1,128)S(1)} collective-permute-done((f32[1,262144]{1,0:T(1,128)S(1)}, f32[1,262144]{1,0:T(1,128)S(1)}, u32[]{:S(2)}, u32[]{:S(2)}) %collective-permute-start.5) | collective-permute-done | bytes 1048608 | tf_op jit(solution)/shard_map/ppermute | solution.py:19
  168.1 25.4 %collective-permute-done.6 = f32[1,262144]{1,0:T(1,128)} collective-permute-done((f32[1,262144]{1,0:T(1,128)S(1)}, f32[1,262144]{1,0:T(1,128)}, u32[]{:S(2)}, u32[]{:S(2)}) %collective-permute-start.6) | collective-permute-done | bytes 1048608 | tf_op jit(solution)/shard_map/ppermute | solution.py:19
  197.0 18.3 %collective-permute-done.7 = f32[1,262144]{1,0:T(1,128)} collective-permute-done((f32[1,262144]{1,0:T(1,128)}, f32[1,262144]{1,0:T(1,128)}, u32[]{:S(2)}, u32[]{:S(2)}) %collective-permute-start.7) | collective-permute-done | bytes 1048608 | tf_op jit(solution)/shard_map/ppermute | solution.py:19
  215.3 13.9 %broadcast_multiply_fusion = (f32[2,262144]{1,0:T(2,128)S(1)}, f32[2,262144]{1,0:T(2,128)S(1)}, f32[2,262144]{1,0:T(2,128)}, f32[2,262144]{1,0:T(2,128)}) fusion(f32[2,262144]{1,0:T(2,128)} %all-gather.2.cloned.1.call-done, f32[262144]{0:T(1024)} %bitcast.125, f32[262144]{0:T(1024)} %bitcast.86, f32[262144]{0:T(1024)} %bitcast.343, f32[262144]{0:T(1024)S(1)} %bitcast.341), kind=kLoop, calls=%fused_computation.105 | loop fusion | flops 2097152 | bytes 14680064 | tf_op jit(solution)/shard_map/mul | solution.py:55
  229.2 13.2 %slice_reduce_fusion.1 = (f32[262144]{0:T(1024)}, f32[262144]{0:T(1024)}, f32[262144]{0:T(1024)}, f32[262144]{0:T(1024)}) fusion(f32[2,262144]{1,0:T(2,128)S(1)} %get-tuple-element.21, f32[2,262144]{1,0:T(2,128)S(1)} %get-tuple-element.22), kind=kLoop, calls=%fused_computation.98 | loop fusion | bytes 8388608 | tf_op jit(solution)/shard_map/slice | solution.py:59
  242.5 2.7 stack.90
  245.1 3.4 copy.67
  248.5 2.7 stack.91
  251.2 3.3 copy.68
  254.5 5.9 fusion.105
  260.4 8.7 %fusion.80 = f32[2,64,64,64,1]{3,2,0,1,4:T(8,128)S(1)} fusion(f32[2,64,64,64,1]{3,2,0,1,4:T(8,128)S(1)} %fusion.105, f32[1,64,2,64]{3,1,2,0:T(8,128)S(1)} %get-tuple-element.28, f32[1,64,2,64]{3,1,2,0:T(8,128)S(1)} %get-tuple-element.27), kind=kOutput, calls=%fused_computation.72 | convolution fusion | flops 805322752 | bytes 4259840 | tf_op jit(solution)/shard_map/qmpa,zpabc->zqbcm/dot_general | solution.py:46
  269.1 8.9 %fusion.29 = f32[2,64,64,64,1]{3,2,0,1,4:T(8,128)S(1)} fusion(f32[2,64,64,64,1]{3,2,0,1,4:T(8,128)S(1)} %fusion.80, f32[64,64,64]{2,1,0:T(8,128)S(1)} %add_divide_fusion, f32[1,64,2,64]{3,1,2,0:T(8,128)S(1)} %get-tuple-element.28, f32[1,64,2,64]{3,1,2,0:T(8,128)S(1)} %get-tuple-element.27), kind=kOutput, calls=%fused_computation.35 | convolution fusion | flops 805847040 | bytes 5308416 | tf_op jit(solution)/shard_map/qmpa,zpabc->zqbcm/dot_general | solution.py:46
  278.1 9.1 %fusion.83 = f32[2,64,64,64,1]{3,2,0,1,4:T(8,128)S(1)} fusion(f32[2,64,64,64,1]{3,2,0,1,4:T(8,128)S(1)} %fusion.29, f32[1,64,2,64]{3,1,2,0:T(8,128)S(1)} %get-tuple-element.26, f32[1,64,2,64]{3,1,2,0:T(8,128)S(1)} %get-tuple-element.25), kind=kOutput, calls=%fused_computation.73 | convolution fusion | flops 805322752 | bytes 4259840 | tf_op jit(solution)/shard_map/qmpa,zpabc->zqbcm/dot_general | solution.py:46
  287.2 8.7 %fusion.86 = f32[2,64,64,64,1]{3,2,0,1,4:T(8,128)S(1)} fusion(f32[2,64,64,64,1]{3,2,0,1,4:T(8,128)S(1)} %fusion.83, f32[1,64,2,64]{3,1,2,0:T(8,128)S(1)} %get-tuple-element.26, f32[1,64,2,64]{3,1,2,0:T(8,128)S(1)} %get-tuple-element.25), kind=kOutput, calls=%fused_computation.74 | convolution fusion | flops 805322752 | bytes 4259840 | tf_op jit(solution)/shard_map/qmpa,zpabc->zqbcm/dot_general | solution.py:46
  295.9 8.6 %fusion.89 = f32[1,2,64,64,64]{4,3,1,2,0:T(8,128)S(1)} fusion(f32[2,64,64,64,1]{3,2,0,1,4:T(8,128)S(1)} %fusion.86, f32[1,64,2,64]{3,1,2,0:T(8,128)S(1)} %get-tuple-element.26, f32[1,64,2,64]{3,1,2,0:T(8,128)S(1)} %get-tuple-element.25), kind=kOutput, calls=%fused_computation.75 | convolution fusion | flops 805322752 | bytes 4259840 | tf_op jit(solution)/shard_map/qmpa,zpabc->zqbcm/dot_general | solution.py:46
  304.5 2.4 fusion.135
  306.8 3.9 concatenate.46
  310.7 3.9 concatenate.47
  314.6 2.7 stack.93
  317.2 3.4 copy.74
  320.6 2.7 stack.94
  323.3 3.3 copy.75
  326.6 6.2 fusion.104
  332.8 8.7 %fusion.92 = f32[2,64,64,64,1]{3,2,0,1,4:T(8,128)S(1)} fusion(f32[2,64,64,64,1]{3,2,0,1,4:T(8,128)S(1)} %fusion.104, f32[1,64,2,64]{3,1,2,0:T(8,128)S(1)} %get-tuple-element.28, f32[1,64,2,64]{3,1,2,0:T(8,128)S(1)} %get-tuple-element.27), kind=kOutput, calls=%fused_computation.76 | convolution fusion | flops 805322752 | bytes 4259840 | tf_op jit(solution)/shard_map/qmpa,zpabc->zqbcm/dot_general | solution.py:46
  341.5 8.9 %fusion.18 = f32[2,64,64,64,1]{3,2,0,1,4:T(8,128)S(1)} fusion(f32[2,64,64,64,1]{3,2,0,1,4:T(8,128)S(1)} %fusion.92, f32[64,64,64]{2,1,0:T(8,128)S(1)} %add_divide_fusion, f32[1,64,2,64]{3,1,2,0:T(8,128)S(1)} %get-tuple-element.28, f32[1,64,2,64]{3,1,2,0:T(8,128)S(1)} %get-tuple-element.27), kind=kOutput, calls=%fused_computation.23 | convolution fusion | flops 805847040 | bytes 5308416 | tf_op jit(solution)/shard_map/qmpa,zpabc->zqbcm/dot_general | solution.py:46
  350.4 8.9 %fusion.95 = f32[2,64,64,64,1]{3,2,0,1,4:T(8,128)S(1)} fusion(f32[2,64,64,64,1]{3,2,0,1,4:T(8,128)S(1)} %fusion.18, f32[1,64,2,64]{3,1,2,0:T(8,128)S(1)} %get-tuple-element.26, f32[1,64,2,64]{3,1,2,0:T(8,128)S(1)} %get-tuple-element.25), kind=kOutput, calls=%fused_computation.77 | convolution fusion | flops 805322752 | bytes 4259840 | tf_op jit(solution)/shard_map/qmpa,zpabc->zqbcm/dot_general | solution.py:46
  359.3 8.4 %fusion.98 = f32[2,64,64,64,1]{3,2,0,1,4:T(8,128)S(1)} fusion(f32[2,64,64,64,1]{3,2,0,1,4:T(8,128)S(1)} %fusion.95, f32[1,64,2,64]{3,1,2,0:T(8,128)S(1)} %get-tuple-element.26, f32[1,64,2,64]{3,1,2,0:T(8,128)S(1)} %get-tuple-element.25), kind=kOutput, calls=%fused_computation.78 | convolution fusion | flops 805322752 | bytes 4259840 | tf_op jit(solution)/shard_map/qmpa,zpabc->zqbcm/dot_general | solution.py:46
  367.7 8.7 %fusion.101 = f32[1,2,64,64,64]{4,3,1,2,0:T(8,128)S(1)} fusion(f32[2,64,64,64,1]{3,2,0,1,4:T(8,128)S(1)} %fusion.98, f32[1,64,2,64]{3,1,2,0:T(8,128)S(1)} %get-tuple-element.26, f32[1,64,2,64]{3,1,2,0:T(8,128)S(1)} %get-tuple-element.25), kind=kOutput, calls=%fused_computation.79 | convolution fusion | flops 805322752 | bytes 4259840 | tf_op jit(solution)/shard_map/qmpa,zpabc->zqbcm/dot_general | solution.py:46
  376.4 2.4 fusion.134
  378.8 3.9 concatenate.49
  382.7 3.9 concatenate.50
  386.6 17.0 %slice_reduce_fusion.5 = (f32[262144]{0:T(1024)}, f32[262144]{0:T(1024)}, f32[262144]{0:T(1024)}, f32[262144]{0:T(1024)}) fusion(f32[2,262144]{1,0:T(2,128)} %get-tuple-element.23, f32[2,262144]{1,0:T(2,128)} %get-tuple-element.24), kind=kLoop, calls=%fused_computation.102 | loop fusion | bytes 8388608 | tf_op jit(solution)/shard_map/slice | solution.py:59
  403.6 2.7 stack.87
  406.3 3.4 copy.60
  409.7 2.7 stack.88
  412.4 3.3 copy.61
  415.8 6.0 fusion.106
  421.7 8.7 %fusion.68 = f32[2,64,64,64,1]{3,2,0,1,4:T(8,128)S(1)} fusion(f32[2,64,64,64,1]{3,2,0,1,4:T(8,128)S(1)} %fusion.106, f32[1,64,2,64]{3,1,2,0:T(8,128)S(1)} %get-tuple-element.28, f32[1,64,2,64]{3,1,2,0:T(8,128)S(1)} %get-tuple-element.27), kind=kOutput, calls=%fused_computation.68 | convolution fusion | flops 805322752 | bytes 4259840 | tf_op jit(solution)/shard_map/qmpa,zpabc->zqbcm/dot_general | solution.py:46
  430.4 9.1 %fusion.40 = f32[2,64,64,64,1]{3,2,0,1,4:T(8,128)S(1)} fusion(f32[2,64,64,64,1]{3,2,0,1,4:T(8,128)S(1)} %fusion.68, f32[64,64,64]{2,1,0:T(8,128)S(1)} %add_divide_fusion, f32[1,64,2,64]{3,1,2,0:T(8,128)S(1)} %get-tuple-element.28, f32[1,64,2,64]{3,1,2,0:T(8,128)S(1)} %get-tuple-element.27), kind=kOutput, calls=%fused_computation.47 | convolution fusion | flops 805847040 | bytes 5308416 | tf_op jit(solution)/shard_map/qmpa,zpabc->zqbcm/dot_general | solution.py:46
  439.6 8.9 %fusion.71 = f32[2,64,64,64,1]{3,2,0,1,4:T(8,128)S(1)} fusion(f32[2,64,64,64,1]{3,2,0,1,4:T(8,128)S(1)} %fusion.40, f32[1,64,2,64]{3,1,2,0:T(8,128)S(1)} %get-tuple-element.26, f32[1,64,2,64]{3,1,2,0:T(8,128)S(1)} %get-tuple-element.25), kind=kOutput, calls=%fused_computation.69 | convolution fusion | flops 805322752 | bytes 4259840 | tf_op jit(solution)/shard_map/qmpa,zpabc->zqbcm/dot_general | solution.py:46
  448.4 8.4 %fusion.74 = f32[2,64,64,64,1]{3,2,0,1,4:T(8,128)S(1)} fusion(f32[2,64,64,64,1]{3,2,0,1,4:T(8,128)S(1)} %fusion.71, f32[1,64,2,64]{3,1,2,0:T(8,128)S(1)} %get-tuple-element.26, f32[1,64,2,64]{3,1,2,0:T(8,128)S(1)} %get-tuple-element.25), kind=kOutput, calls=%fused_computation.70 | convolution fusion | flops 805322752 | bytes 4259840 | tf_op jit(solution)/shard_map/qmpa,zpabc->zqbcm/dot_general | solution.py:46
  456.8 8.7 %fusion.77 = f32[1,2,64,64,64]{4,3,1,2,0:T(8,128)S(1)} fusion(f32[2,64,64,64,1]{3,2,0,1,4:T(8,128)S(1)} %fusion.74, f32[1,64,2,64]{3,1,2,0:T(8,128)S(1)} %get-tuple-element.26, f32[1,64,2,64]{3,1,2,0:T(8,128)S(1)} %get-tuple-element.25), kind=kOutput, calls=%fused_computation.71 | convolution fusion | flops 805322752 | bytes 4259840 | tf_op jit(solution)/shard_map/qmpa,zpabc->zqbcm/dot_general | solution.py:46
  467.8 3.9 concatenate.43
  471.7 4.0 concatenate.44
  475.7 2.7 stack.74
  478.4 3.3 copy.53
  481.7 2.7 stack.75
  484.4 3.3 copy.54
  487.7 5.9 fusion.107
  493.6 8.7 %fusion.56 = f32[2,64,64,64,1]{3,2,0,1,4:T(8,128)S(1)} fusion(f32[2,64,64,64,1]{3,2,0,1,4:T(8,128)S(1)} %fusion.107, f32[1,64,2,64]{3,1,2,0:T(8,128)S(1)} %get-tuple-element.28, f32[1,64,2,64]{3,1,2,0:T(8,128)S(1)} %get-tuple-element.27), kind=kOutput, calls=%fused_computation.64 | convolution fusion | flops 805322752 | bytes 4259840 | tf_op jit(solution)/shard_map/qmpa,zpabc->zqbcm/dot_general | solution.py:46
  502.3 8.9 %fusion.51 = f32[2,64,64,64,1]{3,2,0,1,4:T(8,128)S(1)} fusion(f32[2,64,64,64,1]{3,2,0,1,4:T(8,128)S(1)} %fusion.56, f32[64,64,64]{2,1,0:T(8,128)S(1)} %add_divide_fusion, f32[1,64,2,64]{3,1,2,0:T(8,128)S(1)} %get-tuple-element.28, f32[1,64,2,64]{3,1,2,0:T(8,128)S(1)} %get-tuple-element.27), kind=kOutput, calls=%fused_computation.59 | convolution fusion | flops 805847040 | bytes 5308416 | tf_op jit(solution)/shard_map/qmpa,zpabc->zqbcm/dot_general | solution.py:46
  511.3 9.1 %fusion.59 = f32[2,64,64,64,1]{3,2,0,1,4:T(8,128)S(1)} fusion(f32[2,64,64,64,1]{3,2,0,1,4:T(8,128)S(1)} %fusion.51, f32[1,64,2,64]{3,1,2,0:T(8,128)S(1)} %get-tuple-element.26, f32[1,64,2,64]{3,1,2,0:T(8,128)S(1)} %get-tuple-element.25), kind=kOutput, calls=%fused_computation.65 | convolution fusion | flops 805322752 | bytes 4259840 | tf_op jit(solution)/shard_map/qmpa,zpabc->zqbcm/dot_general | solution.py:46
  520.4 8.7 %fusion.62 = f32[2,64,64,64,1]{3,2,0,1,4:T(8,128)S(1)} fusion(f32[2,64,64,64,1]{3,2,0,1,4:T(8,128)S(1)} %fusion.59, f32[1,64,2,64]{3,1,2,0:T(8,128)S(1)} %get-tuple-element.26, f32[1,64,2,64]{3,1,2,0:T(8,128)S(1)} %get-tuple-element.25), kind=kOutput, calls=%fused_computation.66 | convolution fusion | flops 805322752 | bytes 4259840 | tf_op jit(solution)/shard_map/qmpa,zpabc->zqbcm/dot_general | solution.py:46
  529.1 8.6 %fusion.65 = f32[1,2,64,64,64]{4,3,1,2,0:T(8,128)S(1)} fusion(f32[2,64,64,64,1]{3,2,0,1,4:T(8,128)S(1)} %fusion.62, f32[1,64,2,64]{3,1,2,0:T(8,128)S(1)} %get-tuple-element.26, f32[1,64,2,64]{3,1,2,0:T(8,128)S(1)} %get-tuple-element.25), kind=kOutput, calls=%fused_computation.67 | convolution fusion | flops 805322752 | bytes 4259840 | tf_op jit(solution)/shard_map/qmpa,zpabc->zqbcm/dot_general | solution.py:46
  539.5 3.9 concatenate.40
  543.4 2.3 concatenate.41
  545.7 13.9 %fusion.118 = f32[2,262144]{1,0:T(2,128)} fusion(f32[1,262144]{1,0:T(1,128)} %concatenate.41, f32[1,262144]{1,0:T(1,128)} %concatenate.40, f32[1,262144]{1,0:T(1,128)} %concatenate.44, f32[1,262144]{1,0:T(1,128)} %concatenate.43, f32[1,262144]{1,0:T(1,128)} %concatenate.47, f32[1,262144]{1,0:T(1,128)} %concatenate.46, f32[1,262144]{1,0:T(1,128)} %concatenate.50, ...), kind=kLoop, calls=%fused_computation.87 | loop fusion | flops 5767168 | bytes 14680064 | tf_op jit(solution)/shard_map/add | solution.py:82
  560.9 69.9 %all-reduce.3.cloned.1.call-done = f32[2,262144]{1,0:T(2,128)} async-done(((f32[2,262144]{1,0:T(2,128)}), f32[2,262144]{1,0:T(2,128)}) %all-reduce.3.cloned.1.call-update) | async-done | bytes 2097168
  (36 shorter events, 20.4 us)
Async XLA Ops:
  6.5 190.4 %all-gather.2.cloned.1.call-start = ((), (), s32[]{:S(2)}) async-start(), calls=%async_computation | async-start | bytes 2621440 | tf_op jit(solution)/shard_map/all_gather | solution.py:67
  9.0 30.1 %collective-permute-start = (f32[1,262144]{1,0:T(1,128)S(1)}, f32[1,262144]{1,0:T(1,128)S(1)}, u32[]{:S(2)}, u32[]{:S(2)}) collective-permute-start(f32[1,262144]{1,0:T(1,128)S(1)} %broadcast_multiply_fusion.4), channel_id=1, source_target_pairs={{31,0},{0,1},{1,2},{2,3},{3,4},{4,5},{5,6},{6,7},{7,8},{8,9},{9,10... | collective-permute-start | bytes 3145736 | tf_op jit(solution)/shard_map/ppermute | solution.py:19
  41.3 26.8 %collective-permute-start.1 = (f32[1,262144]{1,0:T(1,128)S(1)}, f32[1,262144]{1,0:T(1,128)S(1)}, u32[]{:S(2)}, u32[]{:S(2)}) collective-permute-start(f32[1,262144]{1,0:T(1,128)S(1)} %broadcast_select_fusion), channel_id=1, source_target_pairs={{30,0},{31,1},{0,2},{1,3},{2,4},{3,5},{4,6},{5,7},{6,8},{7,9},{8,1... | collective-permute-start | bytes 3145736 | tf_op jit(solution)/shard_map/ppermute | solution.py:19
  69.2 26.2 %collective-permute-start.2 = (f32[1,262144]{1,0:T(1,128)S(1)}, f32[1,262144]{1,0:T(1,128)S(1)}, u32[]{:S(2)}, u32[]{:S(2)}) collective-permute-start(f32[1,262144]{1,0:T(1,128)S(1)} %broadcast_select_fusion.1), channel_id=1, source_target_pairs={{28,0},{29,1},{30,2},{31,3},{0,4},{1,5},{2,6},{3,7},{4,8},{5,9},{6... | collective-permute-start | bytes 3145736 | tf_op jit(solution)/shard_map/ppermute | solution.py:19
  96.5 22.9 %collective-permute-start.3 = (f32[1,262144]{1,0:T(1,128)S(1)}, f32[1,262144]{1,0:T(1,128)S(1)}, u32[]{:S(2)}, u32[]{:S(2)}) collective-permute-start(f32[1,262144]{1,0:T(1,128)S(1)} %broadcast_select_fusion.2), channel_id=1, source_target_pairs={{24,0},{25,1},{26,2},{27,3},{28,4},{29,5},{30,6},{31,7},{0,8},{1,9... | collective-permute-start | bytes 3145736 | tf_op jit(solution)/shard_map/ppermute | solution.py:19
  120.5 22.2 %collective-permute-start.4 = (f32[1,262144]{1,0:T(1,128)S(1)}, f32[1,262144]{1,0:T(1,128)S(1)}, u32[]{:S(2)}, u32[]{:S(2)}) collective-permute-start(f32[1,262144]{1,0:T(1,128)S(1)} %broadcast_select_fusion.3), channel_id=1, source_target_pairs={{16,0},{17,1},{18,2},{19,3},{20,4},{21,5},{22,6},{23,7},{24,8},{25... | collective-permute-start | bytes 3145736 | tf_op jit(solution)/shard_map/ppermute | solution.py:19
  143.8 24.0 %collective-permute-start.5 = (f32[1,262144]{1,0:T(1,128)S(1)}, f32[1,262144]{1,0:T(1,128)S(1)}, u32[]{:S(2)}, u32[]{:S(2)}) collective-permute-start(f32[1,262144]{1,0:T(1,128)S(1)} %broadcast_select_fusion.4), channel_id=1, source_target_pairs={{31,0},{0,1},{1,2},{2,3},{3,4},{4,5},{5,6},{6,7},{7,8},{8,9},{9,10... | collective-permute-start | bytes 3145736 | tf_op jit(solution)/shard_map/ppermute | solution.py:19
  143.9 486.8 %all-reduce.3.cloned.1.call-start = ((), (), s32[]{:S(2)}) async-start(), calls=%async_computation.1 | async-start | bytes 4194304
  167.8 28.4 %copy-start = (f32[1,262144]{1,0:T(1,128)}, f32[1,262144]{1,0:T(1,128)S(1)}, u32[]{:S(2)}) copy-start(f32[1,262144]{1,0:T(1,128)S(1)} %collective-permute-done.5) | copy-start | bytes 3145732
  167.9 25.7 %collective-permute-start.6 = (f32[1,262144]{1,0:T(1,128)S(1)}, f32[1,262144]{1,0:T(1,128)}, u32[]{:S(2)}, u32[]{:S(2)}) collective-permute-start(f32[1,262144]{1,0:T(1,128)S(1)} %collective-permute-done.5), channel_id=1, source_target_pairs={{31,0},{0,1},{1,2},{2,3},{3,4},{4,5},{5,6},{6,7},{7,8},{8,9},{9,10... | collective-permute-start | bytes 3145736 | tf_op jit(solution)/shard_map/ppermute | solution.py:19
  193.6 21.7 %collective-permute-start.7 = (f32[1,262144]{1,0:T(1,128)}, f32[1,262144]{1,0:T(1,128)}, u32[]{:S(2)}, u32[]{:S(2)}) collective-permute-start(f32[1,262144]{1,0:T(1,128)} %collective-permute-done.6), channel_id=1, source_target_pairs={{31,0},{0,1},{1,2},{2,3},{3,4},{4,5},{5,6},{6,7},{7,8},{8,9},{9,10... | collective-permute-start | bytes 3145736 | tf_op jit(solution)/shard_map/ppermute | solution.py:19
  545.7 14.0 %copy-start.1 = (u32[128]{0:T(128)S(1)}, u32[128]{0:T(128)}, u32[]{:S(2)}) copy-start(u32[128]{0:T(128)} %constant.142) | copy-start | bytes 1540
Sparse Core Ops, SparseCore 0:
  144.1 42.6 all-gather.1
  559.8 70.9 all-reduce.2
where the time goes:
time: 647 us; the launch traced here: 640 us
  waiting for transfers between devices  259 us (40%)
  matrix products  199 us (31%)
  local copies, waits for them, and re-layouts  119 us (18%)
  other arithmetic  39.6 us (6%)
  between operations  17.7 us (3%)
    dot_general x24, matrix products, transform(): jnp.einsum('qmpa,zpabc->zqbcm', dft_matrix, grid_field, precision=lax.Pre...  199 us
    ppermute x8, waiting for transfers between devices, shifted(): return lax.ppermute(block, axis, route)  189 us
    unnamed x3, waiting for transfers between devices  69.9 us
    another operation x16, local copies, waits for them, and re-layouts, exchange_terms(): packed = jnp.stack([density[:half_count], density[half_count:]], axis=1)  48.2 us
    slice x2, local copies, waits for them, and re-layouts, exchange_terms(): packed = jnp.stack([density[:half_count], density[half_count:]], axis=1)  30.3 us
    concatenate x8, local copies, waits for them, and re-layouts, exchange_terms(): potential = jnp.concatenate([both_parts[:, 0], both_parts[:, 1]], axis=0)  29.6 us
    add x1, other arithmetic, local(): accumulated + exchange_terms(whole_targets, visiting, kernel_grid, forwar...  13.9 us
    mul x1, other arithmetic, exchange_terms(): target_rows[:, None, :] * source_rows[None, :, :]  13.9 us
  transfers between devices with their start and end apart: 10, of which 9 were waited for; matrix products, arithmetic and copies ran while one was open for 0% of the time, Pallas kernels for 0%

commit v1 on v0

v1 whole, which is shorter than its diff:
```python
import functools
import math

import jax
import jax.numpy as jnp
import numpy as np
from jax import lax
from jax.experimental import pallas as pl
from jax.experimental.pallas import tpu as pltpu
from jax.sharding import PartitionSpec as P

NG = 64
LANES = 128
ROWS = NG * NG
HALF = NG // 2
QUARTER = NG // 4
UNROLL = 32

box_length = 16.0
screen_square = 0.25
f32 = jnp.float32
bf16 = jnp.bfloat16


def two_terms(matrix):
    matrix = np.asarray(matrix, np.float32)
    high = matrix.astype(jnp.bfloat16)
    low = (matrix - high.astype(np.float32)).astype(jnp.bfloat16)
    return high, low


def tables():
    count = np.arange(NG)
    angle = 2.0 * np.pi * (count[:, None] * count[None, :] % NG) / NG
    h = np.cos(angle) + np.sin(angle)
    order = np.concatenate([np.arange(0, NG, 2), np.arange(1, NG, 2)])

    def left(matrix):
        high, low = two_terms(matrix)
        return np.concatenate([np.concatenate([high, high], 1), np.concatenate([low, low], 1)], 0)

    high, low = two_terms(np.kron(np.eye(2), h))
    right = np.concatenate([np.concatenate([high, low], 1)] * 2, 0)
    return left(h[:, order]), left(h), left(h[order, :]), right


def kernel_table():
    counter = jnp.arange(NG, dtype=jnp.int32)
    signed = jnp.where(counter < NG // 2, counter, counter - NG).astype(f32)
    wave = 2.0 * math.pi * signed / box_length
    square = wave * wave
    summed = square[:, None, None] + square[None, :, None] + jnp.concatenate([square, square])[None, None, :]
    return (4.0 * math.pi / NG**3 / (summed + screen_square)).reshape(ROWS, LANES)


def split(value):
    high = value.astype(bf16)
    low = (value - high.astype(f32)).astype(bf16)
    return high, low


def left_product(table, value):
    high, low = split(value)
    out = jnp.dot(table, jnp.concatenate([high, low], 0), preferred_element_type=f32)
    return out[:NG] + out[NG:]


def right_product(value, table):
    high, low = split(value)
    out = jnp.dot(jnp.concatenate([high, low], 1), table, preferred_element_type=f32)
    return out[:, :LANES] + out[:, LANES:]


def swap_pairs(first, second):
    low = lax.broadcasted_iota(jnp.int32, first.shape, 1) < NG
    return (
        jnp.where(low, first, pltpu.roll(second, NG, 1)),
        jnp.where(low, pltpu.roll(first, NG, 1), second),
    )


def spread(row):
    turned = pltpu.roll(row, NG, 1)
    low = lax.broadcasted_iota(jnp.int32, row.shape, 1) < NG
    return jnp.concatenate([jnp.where(low, row, turned), jnp.where(low, turned, row)], 0)


def halves(value, index):
    return value[:, LANES * index : LANES * index + LANES]


def stop_body(first, place, fields, row, weight, fwd_y, both_x, inv_y, both_z, *rest):
    if first:
        out, one, two = rest
        before = None
    else:
        before, out, one, two = rest

    def position(step, u):
        return place[step * (UNROLL // QUARTER) + u // QUARTER] + u % QUARTER

    def row_at(x):
        return spread(row[pl.ds(pl.multiple_of(x * HALF, HALF), HALF), :])

    @pl.loop(0, NG // UNROLL)
    def _(step):
        products = []
        for u in range(UNROLL):
            density = fields[pl.ds((step * UNROLL + u) * NG, NG), :] * row_at(position(step, u))
            products.append(density)
        moved = [
            left_product(fwd_y[...], jnp.concatenate(products[u : u + 2], 1)) for u in range(0, UNROLL, 2)
        ]
        for u in range(UNROLL):
            one[pl.ds(position(step, u), NG, NG), :] = halves(moved[u // 2], u % 2)

    @pl.loop(0, NG // UNROLL)
    def _(step):
        moved = []
        for u in range(0, UNROLL, 2):
            k = step * UNROLL + u
            pair = jnp.concatenate([one[pl.ds(k * NG, NG), :], one[pl.ds((k + 1) * NG, NG), :]], 1)
            pair = left_product(both_x[...], pair)
            moved += [halves(pair, 0), halves(pair, 1)]
        plane = right_product(jnp.concatenate(moved, 0), both_z[...])
        plane = plane * weight[pl.ds(step * UNROLL * NG, UNROLL * NG), :]
        plane = right_product(plane, both_z[...])
        for u in range(0, UNROLL, 2):
            k = step * UNROLL + u
            pair = jnp.concatenate([plane[u * NG : (u + 1) * NG], plane[(u + 1) * NG : (u + 2) * NG]], 1)
            pair = left_product(both_x[...], pair)
            two[pl.ds(k, NG, NG), :] = halves(pair, 0)
            two[pl.ds(k + 1, NG, NG), :] = halves(pair, 1)

    @pl.loop(0, NG // UNROLL)
    def _(step):
        moved = []
        for u in range(0, UNROLL, 2):
            planes = [
                two[pl.ds(pl.multiple_of(position(step, v) * NG, NG), NG), :] for v in (u, u + 1)
            ]
            moved.append(left_product(inv_y[...], jnp.concatenate(planes, 1)))
        for u in range(UNROLL):
            value = halves(moved[u // 2], u % 2) * row_at(position(step, u))
            at = pl.ds((step * UNROLL + u) * NG, NG)
            if before is not None:
                value = value + before[at, :]
            out[at, :] = value


def stop(place, fields, row, weight, constants, before):
    vmem = pl.BlockSpec(memory_space=pltpu.VMEM)
    args = [place, fields, row, weight, *constants] + ([] if before is None else [before])
    return pl.pallas_call(
        functools.partial(stop_body, before is None),
        out_shape=jax.ShapeDtypeStruct((ROWS, LANES), f32),
        in_specs=[pl.BlockSpec(memory_space=pltpu.SMEM)] + [vmem] * (len(args) - 1),
        out_specs=vmem,
        scratch_shapes=[pltpu.VMEM((ROWS, LANES), f32), pltpu.VMEM((ROWS, LANES), f32)],
        compiler_params=pltpu.CompilerParams(vmem_limit_bytes=40 * 2**20),
        name="stop",
    )(*args)


def arrange_body(rows, out):
    for x in range(QUARTER):
        pair = [rows[pl.ds(x * NG + t, HALF, 2), :] for t in range(2)]
        even, odd = swap_pairs(*pair)
        out[x * NG : x * NG + HALF, :] = even
        out[x * NG + HALF : (x + 1) * NG, :] = odd


def finish_body(mine, other, out):
    for x in range(QUARTER):
        part = -(mine[x * NG : (x + 1) * NG, :] + other[x * NG : (x + 1) * NG, :])
        for t, value in enumerate(swap_pairs(part[:HALF], part[HALF:])):
            out[pl.ds(x * NG + t, HALF, 2), :] = value


def small(body, *args, name):
    return pl.pallas_call(body, out_shape=jax.ShapeDtypeStruct((ROWS // 4, LANES), f32), name=name)(*args)


def moved(block, axes, route):
    return lax.ppermute(block, axes, route)


def everywhere(block, target):
    route = [(g * 32 + b, (lambda to: to[0] * 32 + to[1])(target(g, b))) for g in range(4) for b in range(32)]
    return lax.ppermute(block, ("grp", "blk"), route)


def pair_shift(block, distance):
    if distance % 16 == 0:
        return block
    return lax.ppermute(block, "blk", [(b, (b + 2 * distance) % 32) for b in range(32)])


def local(targets, sources, occupation, offsets):
    group = lax.axis_index("grp")
    low_z = lax.axis_index("blk") % 2

    rows = targets.reshape(2, 512, LANES).transpose(1, 0, 2).reshape(1024, LANES)
    mine = small(arrange_body, rows, name="arrange")
    far = everywhere(mine, lambda g, b: (g ^ 2, b))
    near = everywhere(jnp.concatenate([mine, far], 0), lambda g, b: (g ^ 1, b))
    fields = jnp.concatenate([mine, far, near], 0)
    place = (group ^ jnp.array([0, 2, 1, 3], jnp.int32)) * QUARTER

    scaled = sources * jnp.sqrt(occupation.astype(f32) * 0.5)[:, None]
    scaled = scaled.reshape(ROWS // 2, LANES)
    offset = lax.dynamic_index_in_dim(offsets, group, 0, keepdims=False)
    own = lax.switch(
        (offset // 2 + 1) % 16, [functools.partial(pair_shift, distance=d) for d in range(16)], scaled
    )

    def cross(block):
        return everywhere(block, lambda g, b: (g ^ 2 if g % 2 else g, b ^ 1))

    crossed = cross(own)
    after = pair_shift(own, 1)
    ahead = pair_shift(own, 15)
    same = jnp.where(offset % 2 == 0, ahead, after)
    last = cross(jnp.where(low_z == 1, after, ahead))

    weight = kernel_table()
    constants = [jnp.asarray(table) for table in tables()]
    total = None
    for row in (own, crossed, same, last):
        total = stop(place, fields, row, weight, constants, total)

    partner = everywhere(total[2048:], lambda g, b: (g ^ 1, b))
    total = total[:2048] + partner
    other = everywhere(total[1024:], lambda g, b: (g ^ 2, b))
    result = small(finish_body, total[:1024], other, name="finish")
    return result.reshape(512, 2, LANES).transpose(1, 0, 2).reshape(2, 65536)


def solution(mesh):
    in_specs = (P("blk", "grp"), P(("grp", "blk"), None), P(("grp", "blk")), P())
    out_specs = P("blk", "grp")
    return jax.shard_map(local, mesh=mesh, in_specs=in_specs, out_specs=out_specs, check_vma=False)
```

time: 647 us -> 124 us (0.19)
  waiting for transfers between devices: 259 us -> 48.8 us
  matrix products: 199 us -> 0 us
  local copies, waits for them, and re-layouts: 119 us -> 4.05 us
  Pallas kernels: 0 us -> 35.2 us
  other arithmetic: 39.6 us -> 5.54 us
  starting transfers between devices: 5.27 us -> 24.7 us
  between operations: 17.7 us -> 3.53 us
    dot_general x24 -> x0, matrix products: 199 us -> none  [transform(): jnp.einsum('qmpa,zpabc->zqbcm', dft_matrix, grid_field, precision=lax.Pre...]
    ppermute x8 -> x9, waiting for transfers between devices: 189 us -> 48.8 us  [the longest x3 24.9 us: pair_shift(): lax.ppermute(block, 'blk', [(b, (b + 2 * distance) % 32) for b in range(3...]
    unnamed x3 -> x0, waiting for transfers between devices: 69.9 us -> none
    another operation x16 -> x0, local copies, waits for them, and re-layouts: 48.2 us -> none  [exchange_terms(): packed = jnp.stack([density[:half_count], density[half_count:]], axis=1)]
    slice x6 -> x2, local copies, waits for them, and re-layouts: 39 us -> 0.96 us  [the longest x1 0.89 us: local(): other = everywhere(total[1024:], lambda g, b: (g ^ 2, b))]
    pallas_call x0 -> x6, Pallas kernels: none -> 35.2 us  [the longest x4 31 us: stop(): pl.pallas_call(functools.partial(stop_body, before is None), out_shape=ja...]
    concatenate x8 -> x0, local copies, waits for them, and re-layouts: 29.6 us -> none  [exchange_terms(): potential = jnp.concatenate([both_parts[:, 0], both_parts[:, 1]], axis=0)]
    ppermute x8 -> x9, starting transfers between devices: 5.23 us -> 24.7 us  [the longest x6 17.6 us: everywhere(): return lax.ppermute(block, ('grp', 'blk'), route)]
  transfers between devices with their start and end apart: 10 -> 9, of which waited for: 9 -> 4; matrix products, arithmetic and copies ran while one was open for 0% -> 3% of each run, Pallas kernels for 0% -> 21%
where the time goes in v1:
time: 124 us; the launch traced here: 122 us
  waiting for transfers between devices  48.8 us (39%)
  Pallas kernels  35.2 us (28%)
  starting transfers between devices  24.7 us (20%)
  other arithmetic  5.54 us (4%)
  local copies, waits for them, and re-layouts  4.05 us (3%)
  between operations  3.53 us (3%)
    pallas_call x4, Pallas kernels, stop(): pl.pallas_call(functools.partial(stop_body, before is None), out_shape=ja...  31 us
    ppermute x3, waiting for transfers between devices, pair_shift(): lax.ppermute(block, 'blk', [(b, (b + 2 * distance) % 32) for b in range(3...  24.9 us
    ppermute x6, waiting for transfers between devices, everywhere(): return lax.ppermute(block, ('grp', 'blk'), route)  23.9 us
    ppermute x6, starting transfers between devices, everywhere(): return lax.ppermute(block, ('grp', 'blk'), route)  17.6 us
    ppermute x3, starting transfers between devices, pair_shift(): lax.ppermute(block, 'blk', [(b, (b + 2 * distance) % 32) for b in range(3...  7.04 us
    pallas_call x2, Pallas kernels, small(): pl.pallas_call(body, out_shape=jax.ShapeDtypeStruct((ROWS // 4, LANES), f...  4.23 us
  transfers between devices with their start and end apart: 9, of which 4 were waited for; matrix products, arithmetic and copies ran while one was open for 3% of the time, Pallas kernels for 21%

profile of v1, /device:TPU:1, one launch (start us, length us, event | category | flops | bytes accessed | tf_op | source)
XLA Modules:
  0.0 121.8 jit_solution(1771826043714289238)
XLA Ops:
  0.0 1.2 %dynamic_slice.4 = s32[1]{0:T(128)} dynamic-slice(s32[4]{0:T(128)} %param.28, s32[]{:T(128)S(6)} %select_n.55), dynamic_slice_sizes={1} | dynamic-slice | bytes 12 | tf_op jit(solution)/shard_map/jit(dynamic_index_in_dim)/dynamic_slice | solution.py:212
  4.6 1.8 %broadcast_multiply_fusion = f32[1,262144]{1,0:T(1,128)S(1)} fusion(f32[1,262144]{1,0:T(1,128)} %param.26, f32[]{:T(128)} %bitcast.4), kind=kLoop, calls=%fused_computation.4 | loop fusion | flops 262144 | bytes 2097156 | tf_op jit(solution)/shard_map/mul | solution.py:210
  6.4 27.2 %conditional.1 = (f32[2048,128]{1,0:T(8,128)S(1)}) conditional(s32[]{:T(128)} %clamp.3, f32[2048,128]{1,0:T(8,128)S(1)} %bitcast.13, f32[2048,128]{1,0:T(8,128)S(1)} %bitcast.14, f32[2048,128]{1,0:T(8,128)S(1)} %bitcast.15, f32[2048,128]{1,0:T(8,128)S(1)} %bitcast.16, f32[2048,128]{1,0:T(8,128)S(1)} %bitcast.17, ...), branch_computations={%region_0.1_spmd, %region_1.2_spmd, %region_2.3_spmd, %region_3.4_... | conditional | bytes 6291504 | solution.py:213
  6.4 2.2 %collective-permute-start.3 = (f32[2048,128]{1,0:T(8,128)S(1)}, f32[2048,128]{1,0:T(8,128)S(1)}, u32[]{:S(2)}, u32[]{:S(2)}) collective-permute-start(f32[2048,128]{1,0:T(8,128)S(1)} %param.4), channel_id=1, source_target_pairs={{0,8},{1,9},{2,10},{3,11},{4,12},{5,13},{6,14},{7,15},{8,16},{9,17... | collective-permute-start | bytes 3145736 | tf_op jit(solution)/shard_map/cond/branch_4_fun/ppermute | solution.py:196
  8.6 24.9 %collective-permute-done.3 = f32[2048,128]{1,0:T(8,128)S(1)} collective-permute-done((f32[2048,128]{1,0:T(8,128)S(1)}, f32[2048,128]{1,0:T(8,128)S(1)}, u32[]{:S(2)}, u32[]{:S(2)}) %collective-permute-start.3) | collective-permute-done | bytes 1048608 | tf_op jit(solution)/shard_map/cond/branch_4_fun/ppermute | solution.py:196
  33.5 0.1 copy.16
  33.5 0.1 collective-permute-start.17
  33.6 4.8 %collective-permute-start.18 = (f32[2048,128]{1,0:T(8,128)S(1)}, f32[2048,128]{1,0:T(8,128)}, u32[]{:S(2)}, u32[]{:S(2)}) collective-permute-start(f32[2048,128]{1,0:T(8,128)S(1)} %get-tuple-element.42.row), channel_id=1, source_target_pairs={{0,30},{1,31},{2,0},{3,1},{4,2},{5,3},{6,4},{7,5},{8,6},{9,7},{10,... | collective-permute-start | bytes 3145736 | tf_op jit(solution)/shard_map/ppermute | solution.py:196
  38.4 2.0 %arrange.1 = f32[1024,128]{1,0:T(8,128)} custom-call(f32[1024,128]{1,0:T(8,128)} %bitcast.29), custom_call_target="tpu_custom_call" | custom-call | tf_op jit(solution)/shard_map/arrange/pallas_call | solution.py:181
  40.4 4.8 %collective-permute-start.15 = (f32[1024,128]{1,0:T(8,128)}, f32[1024,128]{1,0:T(8,128)S(1)}, u32[]{:S(2)}, u32[]{:S(2)}) collective-permute-start(f32[1024,128]{1,0:T(8,128)} %arrange.1), channel_id=1, source_target_pairs={{0,64},{1,65},{2,66},{3,67},{4,68},{5,69},{6,70},{7,71},{8,72},{9,... | collective-permute-start | bytes 1572872 | tf_op jit(solution)/shard_map/ppermute | solution.py:190
  45.3 0.2 collective-permute-start.20
  45.4 0.1 add.77
  45.5 0.1 add.78
  45.6 0.1 add.80
  45.7 0.1 pad_maximum_fusion.2
  45.8 9.3 %collective-permute-done.15 = f32[1024,128]{1,0:T(8,128)S(1)} collective-permute-done((f32[1024,128]{1,0:T(8,128)}, f32[1024,128]{1,0:T(8,128)S(1)}, u32[]{:S(2)}, u32[]{:S(2)}) %collective-permute-start.15) | collective-permute-done | bytes 524320 | tf_op jit(solution)/shard_map/ppermute | solution.py:190
  55.0 1.1 pad_maximum_fusion.1
  56.2 3.5 %collective-permute-start.16 = (f32[2048,128]{1,0:T(8,128)S(1)}, f32[2048,128]{1,0:T(8,128)S(1)}, u32[]{:S(2)}, u32[]{:S(2)}) collective-permute-start(f32[2048,128]{1,0:T(8,128)S(1)} %pad_maximum_fusion.1), channel_id=1, source_target_pairs={{0,32},{1,33},{2,34},{3,35},{4,36},{5,37},{6,38},{7,39},{8,40},{9,... | collective-permute-start | bytes 3145736 | tf_op jit(solution)/shard_map/ppermute | solution.py:190
  59.7 0.0 collective-permute-done.17
  59.7 0.0 collective-permute-done.18
  59.7 1.7 %broadcast_select_fusion = (f32[2048,128]{1,0:T(8,128)S(1)}, f32[2048,128]{1,0:T(8,128)S(1)}) fusion(f32[2048,128]{1,0:T(8,128)} %collective-permute-done.18, f32[2048,128]{1,0:T(8,128)} %collective-permute-done.17, pred[]{:T(512)S(6)} %eq.11, pred[]{:T(512)S(6)} %eq.10), kind=kLoop, calls=%fused_computation.5 | loop fusion | flops 524288 | bytes 4194306 | tf_op jit(solution)/shard_map/jit(_where)/select_n | solution.py:223
  61.3 0.0 copy-start.6
  61.4 0.0 copy-start.4
  61.4 4.8 %collective-permute-start.19 = (f32[2048,128]{1,0:T(8,128)S(1)}, f32[2048,128]{1,0:T(8,128)S(1)}, u32[]{:S(2)}, u32[]{:S(2)}) collective-permute-start(f32[2048,128]{1,0:T(8,128)S(1)} %get-tuple-element.39), channel_id=1, source_target_pairs={{0,1},{1,0},{2,3},{3,2},{4,5},{5,4},{6,7},{7,6},{8,9},{9,8},{10,11... | collective-permute-start | bytes 3145736 | tf_op jit(solution)/shard_map/ppermute | solution.py:190
  66.2 0.6 add_divide_fusion.weight
  66.8 0.0 copy-done.6
  66.8 0.0 copy-start
  66.8 0.0 copy-start.1
  66.8 0.0 copy-start.2
  66.8 0.0 copy-start.3
  66.9 0.0 collective-permute-done.16
  66.9 0.0 copy-done.4
  66.9 0.1 pad_maximum_fusion.fields
  67.0 0.7 copy-done
  67.7 0.0 copy-done.1
  67.7 0.0 copy-done.2
  67.7 0.0 copy-done.3
  67.7 7.8 %stop.4.rest_0_ = f32[4096,128]{1,0:T(8,128)S(1)} custom-call(s32[4]{0:T(128)S(1)} %xor_multiply_fusion.place, f32[4096,128]{1,0:T(8,128)S(1)} %pad_maximum_fusion.fields, f32[2048,128]{1,0:T(8,128)S(1)} %get-tuple-element.42.row, f32[4096,128]{1,0:T(8,128)S(1)} %add_divide_fusion.weight, bf16[128,128]{1,0:T(8,128)(2,1)S(1)} %copy-done.1, ...), custom_call_target="tpu_custom_call" | custom-call | tf_op jit(solution)/shard_map/stop/pallas_call | solution.py:154
  75.6 0.0 collective-permute-done.20.row
  75.6 7.7 %stop.5.rest_0_ = f32[4096,128]{1,0:T(8,128)S(1)} custom-call(s32[4]{0:T(128)S(1)} %xor_multiply_fusion.place, f32[4096,128]{1,0:T(8,128)S(1)} %pad_maximum_fusion.fields, f32[2048,128]{1,0:T(8,128)S(1)} %collective-permute-done.20.row, f32[4096,128]{1,0:T(8,128)S(1)} %add_divide_fusion.weight, bf16[128,128]{1,0:T(8,128)(2,1)S(1)} %copy-done.1, ...), custom_call_target="tpu_custom_call" | custom-call | tf_op jit(solution)/shard_map/stop/pallas_call | solution.py:154
  83.3 7.7 %stop.6.rest_0_ = f32[4096,128]{1,0:T(8,128)S(1)} custom-call(s32[4]{0:T(128)S(1)} %xor_multiply_fusion.place, f32[4096,128]{1,0:T(8,128)S(1)} %pad_maximum_fusion.fields, f32[2048,128]{1,0:T(8,128)S(1)} %get-tuple-element.38.row, f32[4096,128]{1,0:T(8,128)S(1)} %add_divide_fusion.weight, bf16[128,128]{1,0:T(8,128)(2,1)S(1)} %copy-done.1, ...), custom_call_target="tpu_custom_call" | custom-call | tf_op jit(solution)/shard_map/stop/pallas_call | solution.py:154
  91.0 0.0 collective-permute-done.19.row
  91.0 7.7 %stop.7 = f32[4096,128]{1,0:T(8,128)S(1)} custom-call(s32[4]{0:T(128)S(1)} %xor_multiply_fusion.place, f32[4096,128]{1,0:T(8,128)S(1)} %pad_maximum_fusion.fields, f32[2048,128]{1,0:T(8,128)S(1)} %collective-permute-done.19.row, f32[4096,128]{1,0:T(8,128)S(1)} %add_divide_fusion.weight, bf16[128,128]{1,0:T(8,128)(2,1)S(1)} %copy-done.1, ...), custom_call_target="tpu_custom_call" | custom-call | tf_op jit(solution)/shard_map/stop/pallas_call | solution.py:154
  98.7 0.1 slice.17
  98.8 0.1 collective-permute-start.21
  98.9 2.6 %collective-permute-done.21 = f32[2048,128]{1,0:T(8,128)S(1)} collective-permute-done((f32[2048,128]{1,0:T(8,128)S(1)}, f32[2048,128]{1,0:T(8,128)S(1)}, u32[]{:S(2)}, u32[]{:S(2)}) %collective-permute-start.21) | collective-permute-done | bytes 1048608 | tf_op jit(solution)/shard_map/ppermute | solution.py:190
  101.6 0.1 slice_add_fusion
  101.7 0.9 fusion.3
  102.6 4.3 %collective-permute-start.22 = (f32[1024,128]{1,0:T(8,128)S(1)}, f32[1024,128]{1,0:T(8,128)S(1)}, u32[]{:S(2)}, u32[]{:S(2)}) collective-permute-start(f32[1024,128]{1,0:T(8,128)S(1)} %get-tuple-element.40), channel_id=1, source_target_pairs={{0,64},{1,65},{2,66},{3,67},{4,68},{5,69},{6,70},{7,71},{8,72},{9,... | collective-permute-start | bytes 1572872 | tf_op jit(solution)/shard_map/ppermute | solution.py:190
  106.8 12.0 %collective-permute-done.22.other = f32[1024,128]{1,0:T(8,128)S(1)} collective-permute-done((f32[1024,128]{1,0:T(8,128)S(1)}, f32[1024,128]{1,0:T(8,128)S(1)}, u32[]{:S(2)}, u32[]{:S(2)}) %collective-permute-start.22) | collective-permute-done | bytes 524320 | tf_op jit(solution)/shard_map/ppermute | solution.py:190
  118.8 0.0 copy-start.5
  118.8 0.8 copy-done.5
  119.6 2.2 %finish.1 = f32[1024,128]{1,0:T(8,128)} custom-call(f32[1024,128]{1,0:T(8,128)} %get-tuple-element.41.mine, f32[1024,128]{1,0:T(8,128)} %copy-done.5), custom_call_target="tpu_custom_call" | custom-call | tf_op jit(solution)/shard_map/finish/pallas_call | solution.py:181
  (4 shorter events, 0.1 us)
Async XLA Ops:
  6.4 27.1 %collective-permute-start.3 = (f32[2048,128]{1,0:T(8,128)S(1)}, f32[2048,128]{1,0:T(8,128)S(1)}, u32[]{:S(2)}, u32[]{:S(2)}) collective-permute-start(f32[2048,128]{1,0:T(8,128)S(1)} %param.4), channel_id=1, source_target_pairs={{0,8},{1,9},{2,10},{3,11},{4,12},{5,13},{6,14},{7,15},{8,16},{9,17... | collective-permute-start | bytes 3145736 | tf_op jit(solution)/shard_map/cond/branch_4_fun/ppermute | solution.py:196
  33.5 26.1 %collective-permute-start.17 = (f32[2048,128]{1,0:T(8,128)S(1)}, f32[2048,128]{1,0:T(8,128)}, u32[]{:S(2)}, u32[]{:S(2)}) collective-permute-start(f32[2048,128]{1,0:T(8,128)S(1)} %get-tuple-element.42.row), channel_id=1, source_target_pairs={{0,2},{1,3},{2,4},{3,5},{4,6},{5,7},{6,8},{7,9},{8,10},{9,11},{10,... | collective-permute-start | bytes 3145736 | tf_op jit(solution)/shard_map/ppermute | solution.py:196
  33.6 26.0 %collective-permute-start.18 = (f32[2048,128]{1,0:T(8,128)S(1)}, f32[2048,128]{1,0:T(8,128)}, u32[]{:S(2)}, u32[]{:S(2)}) collective-permute-start(f32[2048,128]{1,0:T(8,128)S(1)} %get-tuple-element.42.row), channel_id=1, source_target_pairs={{0,30},{1,31},{2,0},{3,1},{4,2},{5,3},{6,4},{7,5},{8,6},{9,7},{10,... | collective-permute-start | bytes 3145736 | tf_op jit(solution)/shard_map/ppermute | solution.py:196
  40.4 14.6 %collective-permute-start.15 = (f32[1024,128]{1,0:T(8,128)}, f32[1024,128]{1,0:T(8,128)S(1)}, u32[]{:S(2)}, u32[]{:S(2)}) collective-permute-start(f32[1024,128]{1,0:T(8,128)} %arrange.1), channel_id=1, source_target_pairs={{0,64},{1,65},{2,66},{3,67},{4,68},{5,69},{6,70},{7,71},{8,72},{9,... | collective-permute-start | bytes 1572872 | tf_op jit(solution)/shard_map/ppermute | solution.py:190
  45.3 30.3 %collective-permute-start.20 = (f32[2048,128]{1,0:T(8,128)S(1)}, f32[2048,128]{1,0:T(8,128)S(1)}, u32[]{:S(2)}, u32[]{:S(2)}) collective-permute-start(f32[2048,128]{1,0:T(8,128)S(1)} %get-tuple-element.42.row), channel_id=1, source_target_pairs={{0,1},{1,0},{2,3},{3,2},{4,5},{5,4},{6,7},{7,6},{8,9},{9,8},{10,11... | collective-permute-start | bytes 3145736 | tf_op jit(solution)/shard_map/ppermute | solution.py:190
  56.2 10.7 %collective-permute-start.16 = (f32[2048,128]{1,0:T(8,128)S(1)}, f32[2048,128]{1,0:T(8,128)S(1)}, u32[]{:S(2)}, u32[]{:S(2)}) collective-permute-start(f32[2048,128]{1,0:T(8,128)S(1)} %pad_maximum_fusion.1), channel_id=1, source_target_pairs={{0,32},{1,33},{2,34},{3,35},{4,36},{5,37},{6,38},{7,39},{8,40},{9,... | collective-permute-start | bytes 3145736 | tf_op jit(solution)/shard_map/ppermute | solution.py:190
  61.3 5.4 %copy-start.6 = (s32[4]{0:T(128)S(1)}, s32[4]{0:T(128)}, u32[]{:S(2)}) copy-start(s32[4]{0:T(128)} %constant.84.clone) | copy-start | bytes 52
  61.4 5.5 %copy-start.4 = (f32[1024,128]{1,0:T(8,128)S(1)}, f32[1024,128]{1,0:T(8,128)}, u32[]{:S(2)}) copy-start(f32[1024,128]{1,0:T(8,128)} %arrange.1) | copy-start | bytes 1572868
  61.4 29.6 %collective-permute-start.19 = (f32[2048,128]{1,0:T(8,128)S(1)}, f32[2048,128]{1,0:T(8,128)S(1)}, u32[]{:S(2)}, u32[]{:S(2)}) collective-permute-start(f32[2048,128]{1,0:T(8,128)S(1)} %get-tuple-element.39), channel_id=1, source_target_pairs={{0,1},{1,0},{2,3},{3,2},{4,5},{5,4},{6,7},{7,6},{8,9},{9,8},{10,11... | collective-permute-start | bytes 3145736 | tf_op jit(solution)/shard_map/ppermute | solution.py:190
  66.8 0.9 copy-start
  66.8 0.9 copy-start.1
  66.8 0.9 copy-start.2
  66.8 0.9 copy-start.3
  98.8 2.7 %collective-permute-start.21 = (f32[2048,128]{1,0:T(8,128)S(1)}, f32[2048,128]{1,0:T(8,128)S(1)}, u32[]{:S(2)}, u32[]{:S(2)}) collective-permute-start(f32[2048,128]{1,0:T(8,128)S(1)} %slice.17), channel_id=1, source_target_pairs={{0,32},{1,33},{2,34},{3,35},{4,36},{5,37},{6,38},{7,39},{8,40},{9,... | collective-permute-start | bytes 3145736 | tf_op jit(solution)/shard_map/ppermute | solution.py:190
  102.6 16.2 %collective-permute-start.22 = (f32[1024,128]{1,0:T(8,128)S(1)}, f32[1024,128]{1,0:T(8,128)S(1)}, u32[]{:S(2)}, u32[]{:S(2)}) collective-permute-start(f32[1024,128]{1,0:T(8,128)S(1)} %get-tuple-element.40), channel_id=1, source_target_pairs={{0,64},{1,65},{2,66},{3,67},{4,68},{5,69},{6,70},{7,71},{8,72},{9,... | collective-permute-start | bytes 1572872 | tf_op jit(solution)/shard_map/ppermute | solution.py:190
  118.8 0.8 copy-start.5
